TPU v7x, 256 devices: a whole 4x4x8 slice. The times are simulated.
256 devices in a mesh: tm: 32 (over y_lo, z, core), gy: 8 (over y_hi, x).
Axes of the slice: x: 4, y: 4 (y_hi: 2, y_lo: 2; y = y_hi * 2 + y_lo), z: 8, core: 2. Of those that a mesh axis runs over, the one named last changes fastest.
Arguments:
- magnetic: bfloat16 [32, 3, 3, 1024, 1024], P('tm', None, None, 'gy'), may hold values from -6 to 6
- velocity: bfloat16 [32, 3, 1, 1024, 1024], P('tm', None, None, 'gy'), may hold values from -6 to 6
- mode_bin: int32 [1024, 1024], P(None, 'gy'), may hold values from 0 to 127, as said below
- omega_edges: int32 [9], replicated, may hold values from 0 to 32, as said below
Outputs:
- power: float32 [32, 1024, 1024], P('tm', None, 'gy')
- spectrum: float32 [8, 128], replicated
Inputs may be any that keep to these rules, and one draw needn't show every extreme that they name: mode_bin = 16 * p + q, where p is a level of min(kz, 1024 - kz) and q a level of min(ky, 1024 - ky); levels never fall as the wavenumber rises, and every value occurs. `omega_edges`: edges rise strictly, the first 0 and the last 32.
All inputs are finite; a program needn't handle non-finite values.
Results may differ from a plain program's by a relative error of at most 0.004.
The roundings to bfloat16 on the way count: a program that leaves them out, or rounds other values in their place, can miss the bound.
Values may be sent and summed in bfloat16 or wider, within the bound.
No kernel may reach another device: no remote copies, remote signals or barrier semaphores. Data moves between devices by JAX's collectives and lax.ppermute only.
A program may use at most 128 MiB of HBM per device.

v0:
```python
import math
import jax
import jax.numpy as jnp
from jax import lax
from jax.sharding import PartitionSpec as P

NBP = 8
NBQ = 16
NB_W = 8
hall_coef = 1.0
highest = lax.Precision.HIGHEST


def extended(cells, sides, width):
    for axis, dim in sides:
        count = lax.axis_size(axis)
        head = lax.slice_in_dim(cells, 0, width, axis=dim)
        tail = lax.slice_in_dim(cells, cells.shape[dim] - width, cells.shape[dim], axis=dim)
        cells = jnp.concatenate(
            [
                lax.ppermute(tail, axis, [(i, (i + 1) % count) for i in range(count)]),
                cells,
                lax.ppermute(head, axis, [((i + 1) % count, i) for i in range(count)]),
            ],
            axis=dim,
        )
    return cells


def window_taper_for(sample_moments, every_time_sample):
    return 0.5 - 0.5 * jnp.cos(
        2.0 * math.pi * (sample_moments.astype(jnp.float32) + 0.5) / every_time_sample
    )


def temporal_coefficients(angular_frequency, sample_moments, every_time_sample):
    phase_angles = jnp.mod(
        angular_frequency[:, None] * sample_moments[None, :], every_time_sample
    ).astype(jnp.float32)
    angles = 2.0 * math.pi * phase_angles / every_time_sample
    taper_weight = window_taper_for(sample_moments, every_time_sample)[None, :]
    return (
        (taper_weight * jnp.cos(angles)).astype(jnp.bfloat16),
        (-taper_weight * jnp.sin(angles)).astype(jnp.bfloat16),
    )


def dft_tables(length):
    series = jnp.arange(length, dtype=jnp.int32)
    phase_angles = jnp.mod(series[:, None] * series[None, :], length).astype(jnp.float32)
    angles = 2.0 * math.pi * phase_angles / length
    return (jnp.cos(angles).astype(jnp.bfloat16), jnp.sin(angles).astype(jnp.bfloat16))


def z_slope(values):
    return (jnp.roll(values, -1, axis=-1) - jnp.roll(values, 1, axis=-1)) * 0.5


def z_turn(re_part, im_part):
    zcos_tab, zsin_tab = dft_tables(re_part.shape[-1])
    turned_re = jnp.dot(re_part, zcos_tab, preferred_element_type=jnp.float32) + jnp.dot(
        im_part, zsin_tab, preferred_element_type=jnp.float32
    )
    turned_im = jnp.dot(im_part, zcos_tab, preferred_element_type=jnp.float32) - jnp.dot(
        re_part, zsin_tab, preferred_element_type=jnp.float32
    )
    return jnp.stack([turned_re, turned_im]).astype(jnp.bfloat16)


def electric_of(magnetic, velocity, slope_magz, slope_magx):
    inner = magnetic[:, :, 1:-1].astype(jnp.float32)
    x_slope = (
        magnetic[:, :, 2:].astype(jnp.float32) - magnetic[:, :, :-2].astype(jnp.float32)
    ) * 0.5
    mag_x, mag_y, mag_z = (inner[:, 0], inner[:, 1], inner[:, 2])
    cur_x = slope_magz - z_slope(mag_y)
    cur_y = z_slope(mag_x) - x_slope[:, 2]
    cur_z = x_slope[:, 1] - slope_magx
    flow = velocity.astype(jnp.float32)
    vel_x, vel_y, vel_z = (flow[:, 0], flow[:, 1], flow[:, 2])
    elec_x = -(vel_y * mag_z - vel_z * mag_y) + hall_coef * (cur_y * mag_z - cur_z * mag_y)
    elec_y = -(vel_z * mag_x - vel_x * mag_z) + hall_coef * (cur_z * mag_x - cur_x * mag_z)
    elec_z = -(vel_x * mag_y - vel_y * mag_x) + hall_coef * (cur_x * mag_y - cur_y * mag_x)
    return jnp.stack([elec_x, elec_y, elec_z], axis=1)


def body(magnetic, velocity, mode_bin, omega_edges):
    face_rows = jnp.stack([magnetic[:, 2, 1:-1], magnetic[:, 0, 1:-1]], axis=1)
    padded = extended(face_rows, (("gy", 3),), 1)
    slopes = (
        padded[:, :, :, 2:].astype(jnp.float32) - padded[:, :, :, :-2].astype(jnp.float32)
    ) * 0.5
    electric = electric_of(magnetic, velocity, slopes[:, 0], slopes[:, 1]).astype(jnp.bfloat16)
    local_t = electric.shape[0]
    z_count = electric.shape[-1]
    every_time_sample = local_t * lax.axis_size("tm")
    half_count = every_time_sample // 2
    owner_rank = lax.axis_index("tm")
    angular_frequency = owner_rank * local_t + jnp.arange(local_t, dtype=jnp.int32) - half_count
    time_segment = lax.all_gather(electric, "tm", axis=0, tiled=True)
    sample_moments = jnp.arange(time_segment.shape[0], dtype=jnp.int32)
    coefficient_real, coefficient_imaginary = temporal_coefficients(
        angular_frequency, sample_moments, every_time_sample
    )
    re_part = jnp.einsum(
        "wt,tcxyz->wcxyz", coefficient_real, time_segment, preferred_element_type=jnp.float32
    )
    im_part = jnp.einsum(
        "wt,tcxyz->wcxyz", coefficient_imaginary, time_segment, preferred_element_type=jnp.float32
    )
    moved = lax.all_to_all(
        z_turn(re_part.astype(jnp.bfloat16), im_part.astype(jnp.bfloat16)),
        "gy",
        split_axis=5,
        concat_axis=4,
        tiled=True,
    )
    y_count = moved.shape[4]
    ycos_tab, ysin_tab = dft_tables(y_count)
    wave_re = jnp.einsum(
        "wcxyk,yq->wcxqk", moved[0], ycos_tab, preferred_element_type=jnp.float32
    ) + jnp.einsum("wcxyk,yq->wcxqk", moved[1], ysin_tab, preferred_element_type=jnp.float32)
    wave_im = jnp.einsum(
        "wcxyk,yq->wcxqk", moved[1], ycos_tab, preferred_element_type=jnp.float32
    ) - jnp.einsum("wcxyk,yq->wcxqk", moved[0], ysin_tab, preferred_element_type=jnp.float32)
    power_map = jnp.sum(wave_re * wave_re + wave_im * wave_im, axis=(1, 2)) / (
        every_time_sample * y_count * z_count
    )
    kz_local = power_map.shape[2]
    block_rows = min(64, y_count)
    bin_total = NBP * NBQ
    bin_range = jnp.arange(bin_total, dtype=jnp.int32)

    def add_block(step_num, summed):
        row_block = lax.dynamic_slice_in_dim(
            power_map, step_num * block_rows, block_rows, 1
        ).reshape(local_t, block_rows * kz_local)
        bin_ids = lax.dynamic_slice_in_dim(mode_bin, step_num * block_rows, block_rows, 0).reshape(
            block_rows * kz_local
        )
        onehot = (bin_ids[:, None] == bin_range[None, :]).astype(jnp.float32)
        return summed + jnp.dot(row_block, onehot, precision=highest)

    by_mode = lax.fori_loop(
        0, y_count // block_rows, add_block, jnp.zeros((local_t, bin_total), jnp.float32)
    )
    omega = owner_rank * local_t + jnp.arange(local_t, dtype=jnp.int32)
    member = (
        (omega[None, :] >= omega_edges[:-1, None]) & (omega[None, :] < omega_edges[1:, None])
    ).astype(jnp.float32)
    partial_value = jnp.dot(member, by_mode, precision=highest)
    binned = lax.psum(partial_value, ("tm", "gy"))
    spectrum = jnp.log(
        binned * (NB_W * bin_total) / (every_time_sample * y_count * z_count) + 1e-06
    )
    return (power_map, spectrum)


def solution(mesh):
    return jax.shard_map(
        body,
        mesh=mesh,
        in_specs=(
            P("tm", None, None, "gy", None),
            P("tm", None, None, "gy", None),
            P(None, "gy"),
            P(),
        ),
        out_specs=(P("tm", None, "gy"), P()),
        check_vma=False,
    )
```

profile of v0, /device:TPU:1, one launch (start us, length us, event | category | flops | bytes accessed | tf_op | source)
XLA Modules:
  0.0 512.5 jit_solution(18000967554781323091)
XLA Ops:
  8.5 6.0 %collective-permute-start = (bf16[1,2,1,1,1024]{4,3,2,1,0:T(2,128)(2,1)S(1)}, bf16[1,2,1,1,1024]{4,3,2,1,0:T(2,128)(2,1)S(1)}, u32[]{:S(2)}, u32[]{:S(2)}) collective-permute-start(bf16[1,2,1,1,1024]{4,3,2,1,0:T(2,128)(2,1)S(1)} %get-tuple-element.139), channel_id=1, source_target_pairs={{1,0},{2,1},{3,2},{4,3},{5,4},{6,5},{7,6},{0,7},{9,8},{10,9},{11,1... | collective-permute-start | bytes 12296 | tf_op jit(solution)/shard_map/ppermute | solution.py:23
  16.7 3.9 collective-permute-done.1
  23.7 142.3 %all-gather.2.cloned.1.call-done = bf16[32,3,1,128,1024]{4,3,2,1,0:T(8,128)(2,1)} async-done(((bf16[1,3,1,128,1024]{4,3,2,1,0:T(8,128)(2,1)}), bf16[32,3,1,128,1024]{4,3,2,1,0:T(8,128)(2,1)}) %all-gather.2.cloned.1.call-update) | async-done | bytes 25165840 | tf_op jit(solution)/shard_map/all_gather | solution.py:100
  166.0 24.4 %fusion.5 = bf16[1,3,128,1024]{3,0,2,1:T(2,128)(2,1)S(1)} fusion(bf16[32,3,128,1024]{3,2,1,0:T(8,128)(2,1)} %bitcast.97, s32[]{:T(128)S(6)} %sub.139), kind=kOutput, calls=%fused_computation.8 | convolution fusion | flops 25166528 | bytes 25952260 | tf_op jit(solution)/shard_map/wt,tcxyz->wcxyz/dot_general | solution.py:108
  190.5 24.9 %fusion.7 = bf16[1,3,128,1024]{3,0,2,1:T(2,128)(2,1)S(1)} fusion(bf16[32,3,128,1024]{3,2,1,0:T(8,128)(2,1)} %bitcast.98, s32[]{:T(128)S(6)} %sub.139), kind=kOutput, calls=%fused_computation.10 | convolution fusion | flops 25166496 | bytes 25952260 | tf_op jit(solution)/shard_map/wt,tcxyz->wcxyz/dot_general | solution.py:105
  215.4 16.1 %fusion.21 = f32[3,128,1024]{2,1,0:T(8,128)S(1)} fusion(bf16[1,3,128,1024]{3,0,2,1:T(2,128)(2,1)S(1)} %fusion.7), kind=kOutput, calls=%fused_computation.27 | convolution fusion | flops 821035008 | bytes 2359296 | tf_op jit(solution)/shard_map/dot_general | solution.py:64
  231.5 16.1 %fusion.23 = f32[3,128,1024]{2,1,0:T(8,128)S(1)} fusion(bf16[1,3,128,1024]{3,0,2,1:T(2,128)(2,1)S(1)} %fusion.5), kind=kOutput, calls=%fused_computation.28 | convolution fusion | flops 821035008 | bytes 2359296 | tf_op jit(solution)/shard_map/dot_general | solution.py:61
  247.6 16.5 %fusion.42 = bf16[1,1,3,1,128,1024]{5,4,2,3,1,0:T(8,128)(2,1)S(1)} fusion(f32[3,128,1024]{2,1,0:T(8,128)S(1)} %fusion.21, bf16[1,3,128,1024]{3,0,2,1:T(2,128)(2,1)S(1)} %fusion.5), kind=kOutput, calls=%fused_computation.41 | convolution fusion | flops 821821440 | bytes 3145728 | tf_op jit(solution)/shard_map/dot_general | solution.py:64
  264.1 16.3 %fusion.39 = bf16[1,1,3,1,128,1024]{5,4,2,3,1,0:T(8,128)(2,1)S(1)} fusion(f32[3,128,1024]{2,1,0:T(8,128)S(1)} %fusion.23, bf16[1,3,128,1024]{3,0,2,1:T(2,128)(2,1)S(1)} %fusion.7), kind=kOutput, calls=%fused_computation.40 | convolution fusion | flops 821821440 | bytes 3145728 | tf_op jit(solution)/shard_map/dot_general | solution.py:61
  280.6 3.0 copy.44
  283.6 6.7 %all-to-all-start = ((bf16[2,1,3,1,128,1024]{4,0,3,2,1,5:T(2,128)(2,1)}), bf16[2,1,3,1,128,1024]{4,0,3,2,1,5:T(2,128)(2,1)S(1)}, u32[]{:S(2)}, u32[]{:S(2)}) async-start(bf16[2,1,3,1,128,1024]{4,0,3,2,1,5:T(2,128)(2,1)} %copy.44), calls=%async_computation | async-start | bytes 3145728 | tf_op jit(solution)/shard_map/all_to_all | solution.py:111
  290.4 22.9 %all-to-all-done = bf16[2,1,3,1,128,1024]{4,0,3,2,1,5:T(2,128)(2,1)S(1)} async-done(((bf16[2,1,3,1,128,1024]{4,0,3,2,1,5:T(2,128)(2,1)}), bf16[2,1,3,1,128,1024]{4,0,3,2,1,5:T(2,128)(2,1)S(1)}, u32[]{:S(2)}, u32[]{:S(2)}) %all-to-all-start) | async-done | bytes 1572896 | tf_op jit(solution)/shard_map/all_to_all | solution.py:111
  313.3 2.4 copy.45
  315.8 17.9 %fusion.29 = f32[1024,3,128]{2,0,1:T(8,128)S(1)} fusion(bf16[3,1024,128]{2,1,0:T(8,128)(2,1)S(1)} %bitcast.104), kind=kOutput, calls=%fused_computation.31 | convolution fusion | flops 821035008 | bytes 2359296 | tf_op jit(solution)/shard_map/wcxyk,yq->wcxqk/dot_general | solution.py:123
  333.7 18.0 %fusion.19 = f32[1024,3,128]{2,0,1:T(8,128)S(1)} fusion(bf16[3,1024,128]{2,1,0:T(8,128)(2,1)S(1)} %bitcast.105), kind=kOutput, calls=%fused_computation.26 | convolution fusion | flops 821035008 | bytes 2359296 | tf_op jit(solution)/shard_map/wcxyk,yq->wcxqk/dot_general | solution.py:122
  351.6 18.0 %fusion.17 = f32[1024,3,128]{2,0,1:T(8,128)S(1)} fusion(bf16[3,1024,128]{2,1,0:T(8,128)(2,1)S(1)} %bitcast.102), kind=kOutput, calls=%fused_computation.25 | convolution fusion | flops 821035008 | bytes 2359296 | tf_op jit(solution)/shard_map/wcxyk,yq->wcxqk/dot_general | solution.py:125
  369.6 18.0 %add_reduce_fusion = f32[1024,128]{1,0:T(8,128)S(1)} fusion(f32[1024,3,128]{2,0,1:T(8,128)S(1)} %fusion.29, f32[1024,3,128]{2,0,1:T(8,128)S(1)} %fusion.17, f32[1024,3,128]{2,0,1:T(8,128)S(1)} %fusion.19, bf16[3,1024,128]{2,1,0:T(8,128)(2,1)S(1)} %bitcast.103), kind=kOutput, calls=%fused_computation.36 | convolution fusion | flops 823263232 | bytes 6029312 | tf_op jit(solution)/shard_map/wcxyk,yq->wcxqk/dot_general | solution.py:120
  387.7 41.5 %while.14 = (s32[]{:T(128)}, f32[1,128]{1,0:T(1,128)S(1)}, f32[1,1024,128]{2,1,0:T(8,128)S(1)}, s32[1024,128]{1,0:T(8,128)}, s32[]{:T(128)}, /*index=5*/s32[]{:T(128)}, s32[]{:T(128)}, s32[]{:T(128)}) while((s32[]{:T(128)}, f32[1,128]{1,0:T(1,128)S(1)}, f32[1,1024,128]{2,1,0:T(8,128)S(1)}, s32[1024,128]{1,0:T(8,128)}, s32[]{:T(128)}, ...), condition=%wide.region_2.3_spmd.clone, body=%wide.region_1.2_spmd.clone.sunk | while | flops 13631751 | bytes 197789 | solution.py:144
  388.5 1.8 fusion.113
  393.7 1.8 fusion.113
  396.3 1.8 fusion.113
  398.9 1.8 fusion.113
  401.5 1.8 fusion.113
  429.3 75.6 %psum.7 = f32[8,128]{1,0:T(8,128)S(1)} all-reduce(f32[8,128]{1,0:T(8,128)S(1)} %broadcast_multiply_fusion), channel_id=1, replica_groups=mesh['tm'=32,'gy'=8] {'tm','gy'}, use_global_device_ids=true, to_apply=%region_3.4 | all-reduce | flops 1024 | bytes 8192 | tf_op jit(solution)/shard_map/psum | solution.py:152
  (77 shorter events, 39.6 us)
Async XLA Ops:
  7.2 8.7 %copy-start = (bf16[1,3,3,128,1024]{4,3,2,1,0:T(8,128)(2,1)S(1)}, bf16[1,3,3,128,1024]{4,3,2,1,0:T(8,128)(2,1)}, u32[]{:S(2)}) copy-start(bf16[1,3,3,128,1024]{4,3,2,1,0:T(8,128)(2,1)} %param.6) | copy-start | bytes 7077892
  7.2 158.9 %all-gather.2.cloned.1.call-start = ((), (), s32[]{:S(2)}) async-start(), calls=%async_computation.1 | async-start | bytes 25952256 | tf_op jit(solution)/shard_map/all_gather | solution.py:100
  8.5 8.2 %collective-permute-start = (bf16[1,2,1,1,1024]{4,3,2,1,0:T(2,128)(2,1)S(1)}, bf16[1,2,1,1,1024]{4,3,2,1,0:T(2,128)(2,1)S(1)}, u32[]{:S(2)}, u32[]{:S(2)}) collective-permute-start(bf16[1,2,1,1,1024]{4,3,2,1,0:T(2,128)(2,1)S(1)} %get-tuple-element.139), channel_id=1, source_target_pairs={{1,0},{2,1},{3,2},{4,3},{5,4},{6,5},{7,6},{0,7},{9,8},{10,9},{11,1... | collective-permute-start | bytes 12296 | tf_op jit(solution)/shard_map/ppermute | solution.py:23
  14.5 2.0 copy-start.2
  14.5 6.1 %collective-permute-start.1 = (bf16[1,2,1,1,1024]{4,3,2,1,0:T(2,128)(2,1)S(1)}, bf16[1,2,1,1,1024]{4,3,2,1,0:T(2,128)(2,1)S(1)}, u32[]{:S(2)}, u32[]{:S(2)}) collective-permute-start(bf16[1,2,1,1,1024]{4,3,2,1,0:T(2,128)(2,1)S(1)} %get-tuple-element.140), channel_id=1, source_target_pairs={{0,1},{1,2},{2,3},{3,4},{4,5},{5,6},{6,7},{7,0},{8,9},{9,10},{10,1... | collective-permute-start | bytes 12296 | tf_op jit(solution)/shard_map/ppermute | solution.py:21
  280.4 9.9 %copy-start.3 = (s32[9]{0:T(128)S(1)}, s32[9]{0:T(128)}, u32[]{:S(2)}) copy-start(s32[9]{0:T(128)} %param.9) | copy-start | bytes 112
  283.6 29.7 %all-to-all-start = ((bf16[2,1,3,1,128,1024]{4,0,3,2,1,5:T(2,128)(2,1)}), bf16[2,1,3,1,128,1024]{4,0,3,2,1,5:T(2,128)(2,1)S(1)}, u32[]{:S(2)}, u32[]{:S(2)}) async-start(bf16[2,1,3,1,128,1024]{4,0,3,2,1,5:T(2,128)(2,1)} %copy.44), calls=%async_computation | async-start | bytes 3145728 | tf_op jit(solution)/shard_map/all_to_all | solution.py:111
  429.2 76.3 %copy-start.1 = (f32[1,1024,128]{2,1,0:T(8,128)}, f32[1,1024,128]{2,1,0:T(8,128)S(1)}, u32[]{:S(2)}) copy-start(f32[1,1024,128]{2,1,0:T(8,128)S(1)} %get-tuple-element.195) | copy-start | bytes 1572868
Sparse Core Ops, SparseCore 0:
  23.8 142.1 all-gather.1
where the time goes:
time: 518 us; the launch traced here: 513 us
  matrix products  215 us (42%)
  waiting for transfers between devices  169 us (33%)
  blocking collectives  75.6 us (15%)
  local copies, waits for them, and re-layouts  19.7 us (4%)
  between operations  14.5 us (3%)
  starting transfers between devices  12.7 us (2%)
  other arithmetic  5.55 us (1%)
    all_gather x1, waiting for transfers between devices, body(): time_segment = lax.all_gather(electric, 'tm', axis=0, tiled=True)  142 us
    psum x1, blocking collectives, body(): binned = lax.psum(partial_value, ('tm', 'gy'))  75.6 us
    dot_general x16, matrix products, add_block(): return summed + jnp.dot(row_block, onehot, precision=highest)  28.7 us
    dot_general x1, matrix products, body(): jnp.einsum('wt,tcxyz->wcxyz', coefficient_real, time_segment, preferred_e...  24.9 us
    dot_general x1, matrix products, body(): jnp.einsum('wt,tcxyz->wcxyz', coefficient_imaginary, time_segment, prefer...  24.4 us
    all_to_all x1, waiting for transfers between devices, body(): lax.all_to_all(z_turn(re_part.astype(jnp.bfloat16), im_part.astype(jnp.bf...  22.9 us
    dot_general x1, matrix products, body(): jnp.einsum('wcxyk,yq->wcxqk', moved[0], ycos_tab, preferred_element_type=...  18 us
    dot_general x1, matrix products, body(): jnp.einsum('wcxyk,yq->wcxqk', moved[1], ysin_tab, preferred_element_type=...  18 us
  transfers between devices with their start and end apart: 4, of which 3 were waited for; matrix products, arithmetic and copies ran while one was open for 0% of the time, Pallas kernels for 0%

commit v1 on v0

--- a/solution.py
+++ b/solution.py
@@ -1,3 +1,4 @@
+import functools
 import math
 import jax
 import jax.numpy as jnp
@@ -9,6 +10,19 @@
 NB_W = 8
 hall_coef = 1.0
 highest = lax.Precision.HIGHEST
+
+
+def extend_the_tails(raw, mesh_name):
+    block_out = jnp.concatenate(
+        jax.lax.all_to_all(
+            jnp.stack(tuple((raw for _ in range(jax.lax.axis_size(mesh_name))))), mesh_name, 0, 0
+        ),
+        axis=0,
+    )
+    return block_out
+
+
+supply_all_gates = functools.partial(extend_the_tails, mesh_name="tm")
 
 
 def extended(cells, sides, width):
@@ -97,7 +111,7 @@
     half_count = every_time_sample // 2
     owner_rank = lax.axis_index("tm")
     angular_frequency = owner_rank * local_t + jnp.arange(local_t, dtype=jnp.int32) - half_count
-    time_segment = lax.all_gather(electric, "tm", axis=0, tiled=True)
+    time_segment = supply_all_gates(electric)
     sample_moments = jnp.arange(time_segment.shape[0], dtype=jnp.int32)
     coefficient_real, coefficient_imaginary = temporal_coefficients(
         angular_frequency, sample_moments, every_time_sample

time: 518 us -> 939 us (1.81)
  waiting for transfers between devices: 169 us -> 561 us
  blocking collectives: 75.6 us -> 102 us
  between operations: 14.5 us -> 1.1 us
    all_to_all x0 -> x1, waiting for transfers between devices: none -> 543 us  [extend_the_tails(): jax.lax.all_to_all(jnp.stack(tuple((raw for _ in range(jax.lax.axis_size(...]
    all_gather x1 -> x0, waiting for transfers between devices: 142 us -> none  [body(): time_segment = lax.all_gather(electric, 'tm', axis=0, tiled=True)]
    psum x1, blocking collectives: 75.6 us -> 102 us  [body(): binned = lax.psum(partial_value, ('tm', 'gy'))]
    all_to_all x0 -> x1, starting transfers between devices: none -> 11.2 us  [extend_the_tails(): jax.lax.all_to_all(jnp.stack(tuple((raw for _ in range(jax.lax.axis_size(...]
where the time goes in v1:
time: 939 us; the launch traced here: 934 us
  waiting for transfers between devices  561 us (60%)
  matrix products  215 us (23%)
  blocking collectives  102 us (11%)
  local copies, waits for them, and re-layouts  28.5 us (3%)
  starting transfers between devices  21 us (2%)
    all_to_all x1, waiting for transfers between devices, extend_the_tails(): jax.lax.all_to_all(jnp.stack(tuple((raw for _ in range(jax.lax.axis_size(...  543 us
    psum x1, blocking collectives, body(): binned = lax.psum(partial_value, ('tm', 'gy'))  102 us
    dot_general x16, matrix products, add_block(): return summed + jnp.dot(row_block, onehot, precision=highest)  28.7 us
    dot_general x1, matrix products, body(): jnp.einsum('wt,tcxyz->wcxyz', coefficient_real, time_segment, preferred_e...  24.9 us
    dot_general x1, matrix products, body(): jnp.einsum('wt,tcxyz->wcxyz', coefficient_imaginary, time_segment, prefer...  24.3 us
  transfers between devices with their start and end apart: 4, of which 3 were waited for; matrix products, arithmetic and copies ran while one was open for 0% of the time, Pallas kernels for 0%

profile of v1, /device:TPU:1, one launch (start us, length us, event | category | flops | bytes accessed | tf_op | source)
XLA Modules:
  0.0 934.0 jit_solution(10483097301150634521)
XLA Ops:
  1.9 6.0 collective-permute-start
  10.1 3.9 collective-permute-done.1
  16.1 8.7 stack.23
  24.9 11.2 %all-to-all-start = ((bf16[32,1,3,1,128,1024]{5,4,3,2,1,0:T(8,128)(2,1)}), bf16[32,1,3,1,128,1024]{5,4,3,2,1,0:T(8,128)(2,1)}, u32[]{:S(2)}, u32[]{:S(2)}) async-start(bf16[32,1,3,1,128,1024]{5,4,3,2,1,0:T(8,128)(2,1)} %stack.23), calls=%async_computation | async-start | bytes 50331648 | tf_op jit(solution)/shard_map/all_to_all | solution.py:17
  36.1 542.8 %all-to-all-done = bf16[32,1,3,1,128,1024]{5,4,3,2,1,0:T(8,128)(2,1)} async-done(((bf16[32,1,3,1,128,1024]{5,4,3,2,1,0:T(8,128)(2,1)}), bf16[32,1,3,1,128,1024]{5,4,3,2,1,0:T(8,128)(2,1)}, u32[]{:S(2)}, u32[]{:S(2)}) %all-to-all-start) | async-done | bytes 25165856 | tf_op jit(solution)/shard_map/all_to_all | solution.py:17
  578.9 24.3 %fusion.5 = bf16[1,3,128,1024]{3,0,2,1:T(2,128)(2,1)S(1)} fusion(bf16[32,3,128,1024]{3,2,1,0:T(8,128)(2,1)} %bitcast.17, s32[]{:T(128)S(6)} %sub.139), kind=kOutput, calls=%fused_computation.8 | convolution fusion | flops 25166528 | bytes 25952260 | tf_op jit(solution)/shard_map/wt,tcxyz->wcxyz/dot_general | solution.py:122
  603.2 24.9 %fusion.7 = bf16[1,3,128,1024]{3,0,2,1:T(2,128)(2,1)S(1)} fusion(bf16[32,3,128,1024]{3,2,1,0:T(8,128)(2,1)} %bitcast.17, s32[]{:T(128)S(6)} %sub.139), kind=kOutput, calls=%fused_computation.10 | convolution fusion | flops 25166496 | bytes 25952260 | tf_op jit(solution)/shard_map/wt,tcxyz->wcxyz/dot_general | solution.py:119
  628.1 16.1 %fusion.23 = f32[3,128,1024]{2,1,0:T(8,128)S(1)} fusion(bf16[1,3,128,1024]{3,0,2,1:T(2,128)(2,1)S(1)} %fusion.5), kind=kOutput, calls=%fused_computation.28 | convolution fusion | flops 821035008 | bytes 2359296 | tf_op jit(solution)/shard_map/dot_general | solution.py:75
  644.2 16.1 %fusion.21 = f32[3,128,1024]{2,1,0:T(8,128)S(1)} fusion(bf16[1,3,128,1024]{3,0,2,1:T(2,128)(2,1)S(1)} %fusion.7), kind=kOutput, calls=%fused_computation.27 | convolution fusion | flops 821035008 | bytes 2359296 | tf_op jit(solution)/shard_map/dot_general | solution.py:78
  660.3 16.5 %fusion.39 = bf16[1,1,3,1,128,1024]{5,4,2,3,1,0:T(8,128)(2,1)S(1)} fusion(f32[3,128,1024]{2,1,0:T(8,128)S(1)} %fusion.23, bf16[1,3,128,1024]{3,0,2,1:T(2,128)(2,1)S(1)} %fusion.7), kind=kOutput, calls=%fused_computation.40 | convolution fusion | flops 821821440 | bytes 3145728 | tf_op jit(solution)/shard_map/dot_general | solution.py:75
  676.8 16.3 %fusion.42 = bf16[1,1,3,1,128,1024]{5,4,2,3,1,0:T(8,128)(2,1)S(1)} fusion(f32[3,128,1024]{2,1,0:T(8,128)S(1)} %fusion.21, bf16[1,3,128,1024]{3,0,2,1:T(2,128)(2,1)S(1)} %fusion.5), kind=kOutput, calls=%fused_computation.41 | convolution fusion | flops 821821440 | bytes 3145728 | tf_op jit(solution)/shard_map/dot_general | solution.py:78
  693.3 3.0 copy.44
  696.3 3.8 all-to-all-start.1
  700.2 14.5 %all-to-all-done.1 = bf16[2,1,3,1,128,1024]{4,0,3,2,1,5:T(2,128)(2,1)S(1)} async-done(((bf16[2,1,3,1,128,1024]{4,0,3,2,1,5:T(2,128)(2,1)}), bf16[2,1,3,1,128,1024]{4,0,3,2,1,5:T(2,128)(2,1)S(1)}, u32[]{:S(2)}, u32[]{:S(2)}) %all-to-all-start.1) | async-done | bytes 1572896 | tf_op jit(solution)/shard_map/all_to_all | solution.py:125
  714.7 2.4 copy.45
  717.2 18.0 %fusion.19 = f32[1024,3,128]{2,0,1:T(8,128)S(1)} fusion(bf16[3,1024,128]{2,1,0:T(8,128)(2,1)S(1)} %bitcast.108), kind=kOutput, calls=%fused_computation.26 | convolution fusion | flops 821035008 | bytes 2359296 | tf_op jit(solution)/shard_map/wcxyk,yq->wcxqk/dot_general | solution.py:136
  735.2 17.9 %fusion.29 = f32[1024,3,128]{2,0,1:T(8,128)S(1)} fusion(bf16[3,1024,128]{2,1,0:T(8,128)(2,1)S(1)} %bitcast.109), kind=kOutput, calls=%fused_computation.31 | convolution fusion | flops 821035008 | bytes 2359296 | tf_op jit(solution)/shard_map/wcxyk,yq->wcxqk/dot_general | solution.py:137
  753.1 18.0 %fusion.17 = f32[1024,3,128]{2,0,1:T(8,128)S(1)} fusion(bf16[3,1024,128]{2,1,0:T(8,128)(2,1)S(1)} %bitcast.106), kind=kOutput, calls=%fused_computation.25 | convolution fusion | flops 821035008 | bytes 2359296 | tf_op jit(solution)/shard_map/wcxyk,yq->wcxqk/dot_general | solution.py:139
  771.0 18.1 %add_reduce_fusion = f32[1024,128]{1,0:T(8,128)S(1)} fusion(f32[1024,3,128]{2,0,1:T(8,128)S(1)} %fusion.29, f32[1024,3,128]{2,0,1:T(8,128)S(1)} %fusion.17, f32[1024,3,128]{2,0,1:T(8,128)S(1)} %fusion.19, bf16[3,1024,128]{2,1,0:T(8,128)(2,1)S(1)} %bitcast.107), kind=kOutput, calls=%fused_computation.36 | convolution fusion | flops 823263232 | bytes 6029312 | tf_op jit(solution)/shard_map/wcxyk,yq->wcxqk/dot_general | solution.py:134
  789.2 41.7 %while.14 = (s32[]{:T(128)}, f32[1,128]{1,0:T(1,128)S(1)}, f32[1,1024,128]{2,1,0:T(8,128)S(1)}, s32[1024,128]{1,0:T(8,128)}, s32[]{:T(128)}, /*index=5*/s32[]{:T(128)}, s32[]{:T(128)}, s32[]{:T(128)}) while((s32[]{:T(128)}, f32[1,128]{1,0:T(1,128)S(1)}, f32[1,1024,128]{2,1,0:T(8,128)S(1)}, s32[1024,128]{1,0:T(8,128)}, s32[]{:T(128)}, ...), condition=%wide.region_2.3_spmd.clone, body=%wide.region_1.2_spmd.clone.sunk | while | flops 13631751 | bytes 197781 | solution.py:158
  790.0 1.8 fusion.116
  792.6 1.8 fusion.116
  797.8 1.8 fusion.116
  830.9 102.2 %psum.7 = f32[8,128]{1,0:T(8,128)S(1)} all-reduce(f32[8,128]{1,0:T(8,128)S(1)} %broadcast_multiply_fusion), channel_id=1, replica_groups=mesh['tm'=32,'gy'=8] {'tm','gy'}, use_global_device_ids=true, to_apply=%region_3.4 | all-reduce | flops 1024 | bytes 8192 | tf_op jit(solution)/shard_map/psum | solution.py:166
  (77 shorter events, 42.3 us)
Async XLA Ops:
  0.6 8.7 copy-start
  1.9 8.2 collective-permute-start
  7.9 2.0 copy-start.2
  7.9 6.1 collective-permute-start.1
  24.9 554.0 %all-to-all-start = ((bf16[32,1,3,1,128,1024]{5,4,3,2,1,0:T(8,128)(2,1)}), bf16[32,1,3,1,128,1024]{5,4,3,2,1,0:T(8,128)(2,1)}, u32[]{:S(2)}, u32[]{:S(2)}) async-start(bf16[32,1,3,1,128,1024]{5,4,3,2,1,0:T(8,128)(2,1)} %stack.23), calls=%async_computation | async-start | bytes 50331648 | tf_op jit(solution)/shard_map/all_to_all | solution.py:17
  693.1 7.0 copy-start.3
  696.3 18.4 %all-to-all-start.1 = ((bf16[2,1,3,1,128,1024]{4,0,3,2,1,5:T(2,128)(2,1)}), bf16[2,1,3,1,128,1024]{4,0,3,2,1,5:T(2,128)(2,1)S(1)}, u32[]{:S(2)}, u32[]{:S(2)}) async-start(bf16[2,1,3,1,128,1024]{4,0,3,2,1,5:T(2,128)(2,1)} %copy.44), calls=%async_computation.1 | async-start | bytes 3145728 | tf_op jit(solution)/shard_map/all_to_all | solution.py:125
  830.8 102.9 %copy-start.1 = (f32[1,1024,128]{2,1,0:T(8,128)}, f32[1,1024,128]{2,1,0:T(8,128)S(1)}, u32[]{:S(2)}) copy-start(f32[1,1024,128]{2,1,0:T(8,128)S(1)} %get-tuple-element.193) | copy-start | bytes 1572868
